TPU v7x, 128 devices: a whole 4x4x4 slice. The times are simulated.
128 devices in a mesh: cls: 8 (over y, core), mem: 16 (over z, x).
Axes of the slice: x: 4, y: 4, z: 4, core: 2. Of those that a mesh axis runs over, the one named last changes fastest.
Arguments:
- images: bfloat16 [3072, 65536], P(('cls', 'mem')), may hold values from -6 to 6
- owner_group: int32 [3072, 1], P(('cls', 'mem')), may hold values from 0 to 7; in each aligned block of 24 rows (0 to 23, 24 to 47, ...) at most 6 rows name the same one
- bin_in_group: int32 [3072], P(('cls', 'mem')), may hold values from 0 to 7
- defocus: bfloat16 [3072], P(('cls', 'mem')), may hold values from 0.5 to 2
- projections: bfloat16 [64, 65536], P('cls'), may hold values from -6 to 6
- sketch_weight: bfloat16 [64, 48], replicated, may hold values from -0.875 to 0.875
Outputs:
- basis: bfloat16 [8, 64, 65536], P('cls', None, 'mem')
Inputs may be any that keep to these rules, and one draw needn't show every extreme that they name: `owner_group`: in the particles of one device no class group is named more than 6 times, and 6 is reached on some device.
All inputs are finite; a program needn't handle non-finite values.
Results may differ from a plain program's by a relative error of at most 0.012.
The roundings to bfloat16 on the way count: a program that leaves them out, or rounds other values in their place, can miss the bound.
Values may be sent and summed in bfloat16 or wider, within the bound.
A program may use at most 128 MiB of HBM per device.

v0:
```python
import math
import jax
import jax.numpy as jnp
from jax import lax
from jax.sharding import PartitionSpec as P

SIDE = 256
CAP = 6
HI = lax.Precision.HIGHEST


def wave_slice(first, width):
    position = first + jnp.arange(width, dtype=jnp.int32)
    column = position % SIDE
    row_idx = position // SIDE
    fx = jnp.where(column < SIDE // 2, column, column - SIDE).astype(jnp.float32) / SIDE
    fy = jnp.where(row_idx < SIDE // 2, row_idx, row_idx - SIDE).astype(jnp.float32) / SIDE
    return 160.0 * (fx * fx + fy * fy)


def bmm(a, b):
    return jnp.einsum("nij,njk->nik", a, b, precision=HI)


def coefficients(gram, pixels):
    total = jnp.trace(gram, axis1=1, axis2=2)[:, None, None] + 1e-06
    scaled = gram / total
    ident = jnp.eye(gram.shape[1], dtype=jnp.float32)[None]
    first = 1.5 * ident - 0.5 * scaled
    later = bmm(bmm(first, scaled), first)
    second = 1.5 * ident - 0.5 * later
    return bmm(second, first) * jnp.sqrt(pixels / total)


def tree(gram, n_mem, rank, pixels):
    blocks = n_mem
    k = gram.reshape(n_mem, rank, n_mem, rank)
    chain = None
    while True:
        diag = jnp.stack([k[i, :, i, :] for i in range(blocks)])
        c = coefficients(diag, pixels)
        if chain is None:
            chain = c[:, :, None, :]
        else:
            chain = jnp.einsum("nij,njmk->nimk", c, chain, precision=HI)
        if blocks == 1:
            return chain.reshape(rank, n_mem * rank)
        k = jnp.einsum("aij,ajbk->aibk", c, k, precision=HI)
        k = jnp.einsum("aibk,blk->aibl", k, c, precision=HI)
        half = blocks // 2
        k = k.reshape(half, 2, rank, half, 2, rank).sum(axis=(1, 4))
        chain = (
            chain.reshape(half, 2, rank, -1, rank)
            .transpose(0, 2, 1, 3, 4)
            .reshape(half, rank, -1, rank)
        )
        blocks = half


def body(images, owner_group, bin_in_group, defocus, projections, sketch_weight):
    n_cls = lax.axis_size("cls")
    n_mem = lax.axis_size("mem")
    pixels = images.shape[1]
    width = pixels // n_mem
    member = lax.axis_index("mem")
    cls = lax.axis_index("cls")
    p_dev = images.shape[0]
    bins_here = projections.shape[0]
    rank_k = sketch_weight.shape[0]
    owners = owner_group[:, 0]
    onehot = (owners[:, None] == jnp.arange(n_cls, dtype=jnp.int32)[None, :]).astype(jnp.int32)
    before = jnp.cumsum(onehot, axis=0) - onehot
    rank = jnp.sum(onehot * before, axis=1)
    target = owners * CAP + rank
    meta = jnp.stack(
        [target.astype(jnp.float32), defocus.astype(jnp.float32), bin_in_group.astype(jnp.float32)]
    )
    meta = lax.all_gather(meta, ("cls", "mem"), tiled=False).reshape(n_cls, n_mem, 3, p_dev)
    rows = lax.all_to_all(images, "mem", split_axis=1, concat_axis=0, tiled=True)
    rows = rows.reshape(n_mem, p_dev, width)
    mine = lax.dynamic_index_in_dim(meta, cls, 0, keepdims=False)[:, 0]
    select = jnp.arange(n_cls * CAP, dtype=jnp.float32)[None, :, None] == mine[:, None, :]
    sent = jnp.einsum(
        "mti,mip->mtp", select.astype(jnp.bfloat16), rows, preferred_element_type=jnp.float32
    ).astype(jnp.bfloat16)
    sent = (
        sent.reshape(n_mem, n_cls, CAP, width)
        .transpose(1, 0, 2, 3)
        .reshape(n_cls * n_mem * CAP, width)
    )
    got = lax.all_to_all(sent, "cls", split_axis=0, concat_axis=0, tiled=True)
    slot = (cls * CAP + jnp.arange(CAP, dtype=jnp.int32)).astype(jnp.float32)
    pick = (slot[None, None, :, None] == meta[:, :, None, 0, :]).astype(jnp.float32)
    focus = jnp.sum(pick * meta[:, :, None, 1, :], axis=-1).reshape(-1)
    local_bin = jnp.sum(pick * meta[:, :, None, 2, :], axis=-1)
    valid = jnp.sum(pick, axis=-1)
    bins = jnp.arange(bins_here, dtype=jnp.float32)
    table = jnp.where((local_bin[..., None] == bins) & (valid[..., None] > 0.5), 1.0, 0.0)
    table = table.reshape(-1, bins_here).astype(jnp.bfloat16)
    proj = lax.dynamic_slice_in_dim(projections, member * width, width, 1)
    chosen = jnp.dot(table, proj, preferred_element_type=jnp.float32)
    chi = focus[:, None] * wave_slice(member * width, width)[None, :]
    ctf = -math.sqrt(1.01) * jnp.sin(chi + math.atan(0.1))
    residual = (got.astype(jnp.float32) - ctf * chosen).astype(jnp.bfloat16)
    residual = (
        residual.reshape(n_cls, n_mem, CAP, width)
        .transpose(1, 0, 2, 3)
        .reshape(n_mem, n_cls * CAP, width)
    )
    sketch = jnp.einsum(
        "ks,msp->mkp", sketch_weight, residual, preferred_element_type=jnp.float32
    ).astype(jnp.bfloat16)
    sketch = sketch.reshape(n_mem * rank_k, width)
    gram = jnp.einsum("ap,bp->ab", sketch, sketch, preferred_element_type=jnp.float32)
    gram = lax.psum(gram, "mem")
    coef = tree(gram, n_mem, rank_k, float(pixels)).astype(jnp.bfloat16)
    result = jnp.dot(coef, sketch, preferred_element_type=jnp.float32).astype(jnp.bfloat16)
    return result[None]


def solution(mesh):
    in_specs = (
        P(("cls", "mem"), None),
        P(("cls", "mem"), None),
        P(("cls", "mem")),
        P(("cls", "mem")),
        P("cls", None),
        P(),
    )
    out_specs = P("cls", None, "mem")
    return jax.shard_map(body, mesh=mesh, in_specs=in_specs, out_specs=out_specs, check_vma=False)
```

profile of v0, /device:TPU:1, one launch (start us, length us, event | category | flops | bytes accessed | tf_op | source)
XLA Modules:
  0.0 546.3 jit_solution(17044176956349966713)
XLA Ops:
  6.5 4.0 copy.191
  10.6 8.5 %all-to-all-start = ((bf16[24,16,4096]{2,0,1:T(8,128)(2,1)}), bf16[24,16,4096]{2,0,1:T(8,128)(2,1)}, u32[]{:S(2)}, u32[]{:S(2)}) async-start(bf16[24,16,4096]{2,0,1:T(8,128)(2,1)} %bitcast.266), calls=%async_computation | async-start | bytes 6291456 | tf_op jit(solution)/shard_map/all_to_all | solution.py:79
  19.4 96.3 %all-gather.1 = f32[128,3,24]{2,1,0:T(4,128)S(1)} all-gather(f32[1,3,24]{2,1,0:T(4,128)S(1)} %maximum_bitcast_fusion), channel_id=2, replica_groups=mesh['cls'=8,'mem'=16] {'cls','mem'}, dimensions={0}, use_global_device_ids=true | all-gather | bytes 37152 | tf_op jit(solution)/shard_map/all_gather | solution.py:78
  115.8 3.8 convolution_convert_fusion.1
  119.6 3.4 copy.115
  123.1 3.4 copy.116
  126.5 6.3 %copy.117 = bf16[8,96,4096]{2,1,0:T(8,128)(2,1)} copy(bf16[8,96,4096]{2,0,1:T(8,128)(2,1)S(1)} %bitcast.264) | data formatting | bytes 12582912 | tf_op jit(solution)/shard_map/all_to_all | solution.py:91
  132.8 5.8 %all-to-all-start.1 = ((bf16[8,96,4096]{2,1,0:T(8,128)(2,1)}), bf16[8,96,4096]{2,1,0:T(8,128)(2,1)}, u32[]{:S(2)}, u32[]{:S(2)}) async-start(bf16[8,96,4096]{2,1,0:T(8,128)(2,1)} %copy.117), calls=%async_computation.1 | async-start | bytes 12582912 | tf_op jit(solution)/shard_map/all_to_all | solution.py:91
  140.1 69.9 %all-to-all-done.1 = bf16[8,96,4096]{2,1,0:T(8,128)(2,1)} async-done(((bf16[8,96,4096]{2,1,0:T(8,128)(2,1)}), bf16[8,96,4096]{2,1,0:T(8,128)(2,1)}, u32[]{:S(2)}, u32[]{:S(2)}) %all-to-all-start.1) | async-done | bytes 6291488 | tf_op jit(solution)/shard_map/all_to_all | solution.py:91
  210.0 47.5 %fusion = bf16[768,4096]{1,0:T(8,128)(2,1)} fusion(bf16[768,4096]{1,0:T(8,128)(2,1)} %bitcast.88, f32[4096]{0:T(1024)S(1)} %fusion.85, f32[768]{0:T(1024)S(1)} %mul.219, f32[768]{0:T(1024)S(1)} %eq.134, pred[768]{0:T(1024)(128)(4,1)S(1)} %gt.16, bf16[8,65536]{1,0:T(8,128)(2,1)S(1)} %copy-done, s32[]{:T(128)S(6)} %select_n.80), kind=kOutput, calls=%fused_computation.1 | convolution fusion | flops 72376320 | bytes 12674052 | tf_op jit(solution)/shard_map/dot_general | solution.py:101
  257.5 10.1 %reshape.271 = bf16[8,16,6,4096]{3,2,1,0:T(8,128)(2,1)} reshape(bf16[768,4096]{1,0:T(8,128)(2,1)} %fusion) | data formatting | bytes 12582912 | tf_op jit(solution)/shard_map/reshape | solution.py:106
  267.7 7.0 %copy.125 = bf16[16,8,6,4096]{3,0,2,1:T(8,128)(2,1)S(1)} copy(bf16[16,8,6,4096]{3,2,0,1:T(8,128)(2,1)} %bitcast.261) | data formatting | bytes 12582912 | tf_op jit(solution)/shard_map/transpose | solution.py:107
  274.6 5.7 %convolution_convert_fusion = bf16[16,4096,64]{1,2,0:T(8,128)(2,1)S(1)} fusion(bf16[16,48,4096]{2,0,1:T(8,128)(2,1)S(1)} %bitcast.265, bf16[64,48]{0,1:T(8,128)(2,1)S(1)} %copy-done.4), kind=kOutput, calls=%fused_computation.4 | convolution fusion | flops 406847488 | bytes 14686208 | tf_op jit(solution)/shard_map/ks,msp->mkp/dot_general | solution.py:110
  280.3 3.2 copy-done.2
  283.5 10.8 %fusion.140 = f32[1024,1024]{1,0:T(8,128)} fusion(bf16[1024,4096]{1,0:T(8,128)(2,1)S(1)} %bitcast.259), kind=kOutput, calls=%fused_computation.242 | convolution fusion | flops 8589934592 | bytes 12582912 | tf_op jit(solution)/shard_map/ap,bp->ab/dot_general | solution.py:114
  294.3 7.3 %reshape.274 = f32[16,64,16,64]{3,2,1,0:T(8,128)} reshape(f32[1024,1024]{1,0:T(8,128)} %fusion.140) | data formatting | bytes 8388608 | tf_op jit(solution)/shard_map/reshape | solution.py:37
  301.6 9.2 %copy.127 = f32[16,64,16,64]{3,1,2,0:T(8,128)} copy(f32[16,64,16,64]{3,2,1,0:T(8,128)} %reshape.274) | data formatting | bytes 8388608 | tf_op jit(solution)/shard_map/reshape | solution.py:37
  310.9 139.2 %all-reduce.2.cloned.1.call-done = f32[16,64,16,64]{3,1,2,0:T(8,128)} async-done(((f32[16,64,16,64]{3,1,2,0:T(8,128)}), f32[16,64,16,64]{3,1,2,0:T(8,128)}) %all-reduce.2.cloned.1.call-update) | async-done | bytes 4194320 | tf_op jit(solution)/shard_map/psum | solution.py:115
  450.1 0.9 constant_dynamic-update-slice_fusion.15
  451.0 0.9 constant_dynamic-update-slice_fusion.14
  451.9 1.1 constant_dynamic-update-slice_fusion.13
  463.1 0.8 fusion.19
  465.3 8.7 %fusion.1 = f32[16,64,16,64]{3,1,0,2:T(8,128)S(1)} fusion(f32[16,64,16,64]{3,1,2,0:T(8,128)S(1)} %copy-done.3, f32[16,64,64]{2,1,0:T(8,128)S(1)} %convolution_multiply_fusion), kind=kOutput, calls=%fused_computation.2 | convolution fusion | flops 805306368 | bytes 8650752 | tf_op jit(solution)/shard_map/aij,ajbk->aibk/dot_general | solution.py:48
  474.0 26.4 %fusion.16 = f32[16,64,16,64]{3,1,2,0:T(8,128)} fusion(f32[16,64,16,64]{3,1,0,2:T(8,128)S(1)} %fusion.1, f32[16,64,64]{2,1,0:T(8,128)S(1)} %convolution_multiply_fusion), kind=kOutput, calls=%fused_computation.36 | convolution fusion | flops 805306368 | bytes 8650752 | tf_op jit(solution)/shard_map/aibk,blk->aibl/dot_general | solution.py:49
  500.4 4.6 reduce_sum.131
  507.4 6.1 %fusion.28 = f32[8,64,8,64]{3,1,0,2:T(8,128)S(1)} fusion(f32[8,64,8,64]{1,3,0,2:T(8,128)S(1)} %reduce_sum.131, f32[8,64,64]{2,1,0:T(8,128)S(1)} %convolution_multiply_fusion.2), kind=kOutput, calls=%fused_computation.53 | convolution fusion | flops 201326592 | bytes 2228224 | tf_op jit(solution)/shard_map/aij,ajbk->aibk/dot_general | solution.py:48
  513.5 1.4 fusion.24
  514.8 6.0 %fusion.26 = f32[8,64,8,64]{3,1,2,0:T(8,128)S(1)} fusion(f32[8,64,8,64]{3,1,0,2:T(8,128)S(1)} %fusion.28, f32[8,64,64]{2,1,0:T(8,128)S(1)} %convolution_multiply_fusion.2), kind=kOutput, calls=%fused_computation.51 | convolution fusion | flops 201326592 | bytes 2228224 | tf_op jit(solution)/shard_map/aibk,blk->aibl/dot_general | solution.py:49
  522.7 1.6 fusion.46
  524.3 1.9 fusion.14
  526.2 1.6 fusion.42
  533.3 5.7 %fusion.4 = bf16[1,64,4096]{2,1,0:T(8,128)(2,1)} fusion(bf16[64,1024]{1,0:T(8,128)(2,1)S(1)} %convolution_convert_fusion.3, bf16[1024,4096]{1,0:T(8,128)(2,1)} %bitcast.260), kind=kOutput, calls=%fused_computation.8 | convolution fusion | flops 537133056 | bytes 9043968 | tf_op jit(solution)/shard_map/dot_general | solution.py:117
  (111 shorter events, 22.0 us)
Async XLA Ops:
  6.5 203.5 %copy-start = (bf16[8,65536]{1,0:T(8,128)(2,1)S(1)}, bf16[8,65536]{1,0:T(8,128)(2,1)}, u32[]{:S(2)}) copy-start(bf16[8,65536]{1,0:T(8,128)(2,1)} %param.10) | copy-start | bytes 3145732
  6.5 12.5 %copy-start.5 = (s32[24,1]{0,1:T(1,128)S(1)}, s32[24,1]{0,1:T(1,128)}, u32[]{:S(2)}) copy-start(s32[24,1]{0,1:T(1,128)} %param.7) | copy-start | bytes 292
  6.5 12.8 %copy-start.6 = (s32[24]{0:T(128)S(1)}, s32[24]{0:T(128)}, u32[]{:S(2)}) copy-start(s32[24]{0:T(128)} %param.8) | copy-start | bytes 292
  6.5 12.9 %copy-start.7 = (bf16[24]{0:T(256)(128)(2,1)S(1)}, bf16[24]{0:T(256)(128)(2,1)}, u32[]{:S(2)}) copy-start(bf16[24]{0:T(256)(128)(2,1)} %param.9) | copy-start | bytes 148
  10.6 105.2 %all-to-all-start = ((bf16[24,16,4096]{2,0,1:T(8,128)(2,1)}), bf16[24,16,4096]{2,0,1:T(8,128)(2,1)}, u32[]{:S(2)}, u32[]{:S(2)}) async-start(bf16[24,16,4096]{2,0,1:T(8,128)(2,1)} %bitcast.266), calls=%async_computation | async-start | bytes 6291456 | tf_op jit(solution)/shard_map/all_to_all | solution.py:79
  132.8 77.2 %all-to-all-start.1 = ((bf16[8,96,4096]{2,1,0:T(8,128)(2,1)}), bf16[8,96,4096]{2,1,0:T(8,128)(2,1)}, u32[]{:S(2)}, u32[]{:S(2)}) async-start(bf16[8,96,4096]{2,1,0:T(8,128)(2,1)} %copy.117), calls=%async_computation.1 | async-start | bytes 12582912 | tf_op jit(solution)/shard_map/all_to_all | solution.py:91
  138.6 311.4 %all-reduce.2.cloned.1.call-start = ((), (), s32[]{:S(2)}) async-start(), calls=%async_computation.2 | async-start | bytes 16777216 | tf_op jit(solution)/shard_map/psum | solution.py:115
  267.6 7.0 %copy-start.4 = (bf16[64,48]{0,1:T(8,128)(2,1)S(1)}, bf16[64,48]{0,1:T(8,128)(2,1)}, u32[]{:S(2)}) copy-start(bf16[64,48]{0,1:T(8,128)(2,1)} %param.11) | copy-start | bytes 18436
  280.3 3.2 copy-start.2
  450.1 15.3 %copy-start.3 = (f32[16,64,16,64]{3,1,2,0:T(8,128)S(1)}, f32[16,64,16,64]{3,1,2,0:T(8,128)}, u32[]{:S(2)}) copy-start(f32[16,64,16,64]{3,1,2,0:T(8,128)} %all-reduce.2.cloned.1.call-done) | copy-start | bytes 12582916
  530.4 8.6 %copy-start.1 = (bf16[8,65536]{1,0:T(8,128)(2,1)S(1)}, bf16[8,65536]{1,0:T(8,128)(2,1)}, u32[]{:S(2)}) copy-start(bf16[8,65536]{1,0:T(8,128)(2,1)} %param.10) | copy-start | bytes 3145732
Sparse Core Ops, SparseCore 0:
  310.9 139.0 all-reduce.1
where the time goes:
time: 557 us; the launch traced here: 546 us
  waiting for transfers between devices  209 us (38%)
  matrix products  135 us (24%)
  blocking collectives  96.3 us (17%)
  local copies, waits for them, and re-layouts  69.5 us (12%)
  between operations  15.1 us (3%)
  starting transfers between devices  14.3 us (3%)
  other arithmetic  7.06 us (1%)
    psum x1, waiting for transfers between devices, body(): gram = lax.psum(gram, 'mem')  139 us
    all_gather x1, blocking collectives, body(): lax.all_gather(meta, ('cls', 'mem'), tiled=False)  96.3 us
    all_to_all x1, waiting for transfers between devices, body(): got = lax.all_to_all(sent, 'cls', split_axis=0, concat_axis=0, tiled=True)  69.9 us
    dot_general x1, matrix products, body(): chosen = jnp.dot(table, proj, preferred_element_type=jnp.float32)  47.5 us
    dot_general x4, matrix products, tree(): k = jnp.einsum('aibk,blk->aibl', k, c, precision=HI)  34.3 us
    dot_general x4, matrix products, tree(): k = jnp.einsum('aij,ajbk->aibk', c, k, precision=HI)  16.8 us
    reshape x2, local copies, waits for them, and re-layouts, tree(): k = gram.reshape(n_mem, rank, n_mem, rank)  16.5 us
    unnamed x52, local copies, waits for them, and re-layouts  16.4 us
  transfers between devices with their start and end apart: 3, of which 2 were waited for; matrix products, arithmetic and copies ran while one was open for 0% of the time, Pallas kernels for 0%

commit v1 on v0

--- a/solution.py
+++ b/solution.py
@@ -112,7 +112,7 @@
     ).astype(jnp.bfloat16)
     sketch = sketch.reshape(n_mem * rank_k, width)
     gram = jnp.einsum("ap,bp->ab", sketch, sketch, preferred_element_type=jnp.float32)
-    gram = lax.psum(gram, "mem")
+    gram = jnp.sum(lax.all_gather(gram, "mem"), axis=0)
     coef = tree(gram, n_mem, rank_k, float(pixels)).astype(jnp.bfloat16)
     result = jnp.dot(coef, sketch, preferred_element_type=jnp.float32).astype(jnp.bfloat16)
     return result[None]

time: 557 us -> 789 us (1.42)
  waiting for transfers between devices: 209 us -> 437 us
  other arithmetic: 7.06 us -> 30 us
  local copies, waits for them, and re-layouts: 69.5 us -> 50.4 us
    all_gather x0 -> x1, waiting for transfers between devices: none -> 367 us  [body(): gram = jnp.sum(lax.all_gather(gram, 'mem'), axis=0)]
    psum x1 -> x0, waiting for transfers between devices: 139 us -> none  [body(): gram = lax.psum(gram, 'mem')]
    reduce_sum x0 -> x1, other arithmetic: none -> 22.9 us  [body(): gram = jnp.sum(lax.all_gather(gram, 'mem'), axis=0)]
    unnamed x52, local copies, waits for them, and re-layouts: 16.4 us -> 4.45 us
    reshape x2 -> x1, local copies, waits for them, and re-layouts: 16.5 us -> 7.24 us  [tree(): k = gram.reshape(n_mem, rank, n_mem, rank)]
where the time goes in v1:
time: 789 us; the launch traced here: 780 us
  waiting for transfers between devices  437 us (55%)
  matrix products  137 us (17%)
  blocking collectives  96.3 us (12%)
  local copies, waits for them, and re-layouts  50.4 us (6%)
  other arithmetic  30 us (4%)
  between operations  15.2 us (2%)
  starting transfers between devices  14.3 us (2%)
    all_gather x1, waiting for transfers between devices, body(): gram = jnp.sum(lax.all_gather(gram, 'mem'), axis=0)  367 us
    all_gather x1, blocking collectives, body(): lax.all_gather(meta, ('cls', 'mem'), tiled=False)  96.3 us
    all_to_all x1, waiting for transfers between devices, body(): got = lax.all_to_all(sent, 'cls', split_axis=0, concat_axis=0, tiled=True)  69.9 us
    dot_general x1, matrix products, body(): chosen = jnp.dot(table, proj, preferred_element_type=jnp.float32)  47.5 us
    dot_general x4, matrix products, tree(): k = jnp.einsum('aibk,blk->aibl', k, c, precision=HI)  34.3 us
    reduce_sum x1, other arithmetic, body(): gram = jnp.sum(lax.all_gather(gram, 'mem'), axis=0)  22.9 us
    dot_general x4, matrix products, tree(): k = jnp.einsum('aij,ajbk->aibk', c, k, precision=HI)  18.9 us
  transfers between devices with their start and end apart: 3, of which 2 were waited for; matrix products, arithmetic and copies ran while one was open for 0% of the time, Pallas kernels for 0%

profile of v1, /device:TPU:1, one launch (start us, length us, event | category | flops | bytes accessed | tf_op | source)
XLA Modules:
  0.0 779.7 jit_solution(6733950433713137099)
XLA Ops:
  6.5 4.0 copy.280
  10.6 8.5 %all-to-all-start = ((bf16[24,16,4096]{2,0,1:T(8,128)(2,1)}), bf16[24,16,4096]{2,0,1:T(8,128)(2,1)}, u32[]{:S(2)}, u32[]{:S(2)}) async-start(bf16[24,16,4096]{2,0,1:T(8,128)(2,1)} %bitcast.251), calls=%async_computation | async-start | bytes 6291456 | tf_op jit(solution)/shard_map/all_to_all | solution.py:79
  19.4 96.3 %all-gather.2 = f32[128,3,24]{2,1,0:T(4,128)S(1)} all-gather(f32[1,3,24]{2,1,0:T(4,128)S(1)} %maximum_bitcast_fusion), channel_id=2, replica_groups=mesh['cls'=8,'mem'=16] {'cls','mem'}, dimensions={0}, use_global_device_ids=true | all-gather | bytes 37152 | tf_op jit(solution)/shard_map/all_gather | solution.py:78
  115.8 3.8 convolution_convert_fusion.1
  119.6 3.4 copy.173
  123.1 3.4 copy.174
  126.5 6.3 copy.175
  132.8 5.8 all-to-all-start.1
  140.1 69.9 %all-to-all-done.1 = bf16[8,96,4096]{2,1,0:T(8,128)(2,1)} async-done(((bf16[8,96,4096]{2,1,0:T(8,128)(2,1)}), bf16[8,96,4096]{2,1,0:T(8,128)(2,1)}, u32[]{:S(2)}, u32[]{:S(2)}) %all-to-all-start.1) | async-done | bytes 6291488 | tf_op jit(solution)/shard_map/all_to_all | solution.py:91
  210.0 47.5 %fusion = bf16[768,4096]{1,0:T(8,128)(2,1)} fusion(bf16[768,4096]{1,0:T(8,128)(2,1)} %bitcast.89, f32[4096]{0:T(1024)S(1)} %fusion.85, f32[768]{0:T(1024)S(1)} %mul.219, f32[768]{0:T(1024)S(1)} %eq.134, pred[768]{0:T(1024)(128)(4,1)S(1)} %gt.16, bf16[8,65536]{1,0:T(8,128)(2,1)S(1)} %copy-done, s32[]{:T(128)S(6)} %select_n.80), kind=kOutput, calls=%fused_computation.1 | convolution fusion | flops 72376320 | bytes 12674052 | tf_op jit(solution)/shard_map/dot_general | solution.py:101
  257.5 10.1 %reshape.271 = bf16[8,16,6,4096]{3,2,1,0:T(8,128)(2,1)} reshape(bf16[768,4096]{1,0:T(8,128)(2,1)} %fusion) | data formatting | bytes 12582912 | tf_op jit(solution)/shard_map/reshape | solution.py:106
  267.7 7.0 copy.183
  274.6 5.7 convolution_convert_fusion
  280.3 3.2 copy-done.3
  283.5 10.8 %fusion.141 = f32[1024,1024]{1,0:T(8,128)} fusion(bf16[1024,4096]{1,0:T(8,128)(2,1)S(1)} %bitcast.244), kind=kOutput, calls=%fused_computation.227 | convolution fusion | flops 8589934592 | bytes 12582912 | tf_op jit(solution)/shard_map/ap,bp->ab/dot_general | solution.py:114
  294.3 366.6 %all-gather.5.cloned.1.call-done = f32[16384,1024]{1,0:T(8,128)} async-done(((f32[1024,1024]{1,0:T(8,128)}), f32[16384,1024]{1,0:T(8,128)}) %all-gather.5.cloned.1.call-update) | async-done | bytes 67108880 | tf_op jit(solution)/shard_map/all_gather | solution.py:115
  661.0 22.9 %reduce_sum.139 = f32[1024,1024]{1,0:T(8,128)} reduce(f32[16,1024,1024]{2,1,0:T(8,128)} %bitcast.22, f32[]{:T(128)} %constant.62.clone.1), dimensions={0}, to_apply=%region_5.6 | reduce | flops 15728640 | bytes 71303168 | tf_op jit(solution)/shard_map/reduce_sum | solution.py:115
  683.9 7.2 reshape.274
  691.1 2.8 fusion.136
  694.4 0.8 fusion.19
  695.2 0.7 fusion.6
  695.9 0.7 convolution_multiply_fusion
  696.7 10.7 %fusion.1 = f32[16,64,16,64]{3,1,0,2:T(8,128)S(1)} fusion(f32[16,64,16,64]{3,2,1,0:T(8,128)S(1)} %copy-done.2, f32[16,64,64]{2,1,0:T(8,128)S(1)} %convolution_multiply_fusion), kind=kOutput, calls=%fused_computation.2 | convolution fusion | flops 805306368 | bytes 8650752 | tf_op jit(solution)/shard_map/aij,ajbk->aibk/dot_general | solution.py:48
  707.4 26.4 %fusion.16 = f32[16,64,16,64]{3,1,2,0:T(8,128)} fusion(f32[16,64,16,64]{3,1,0,2:T(8,128)S(1)} %fusion.1, f32[16,64,64]{2,1,0:T(8,128)S(1)} %convolution_multiply_fusion), kind=kOutput, calls=%fused_computation.36 | convolution fusion | flops 805306368 | bytes 8650752 | tf_op jit(solution)/shard_map/aibk,blk->aibl/dot_general | solution.py:49
  733.7 4.6 reduce_sum.141
  740.7 6.1 fusion.28
  746.8 1.4 fusion.24
  748.2 6.0 fusion.26
  756.0 1.6 fusion.46
  757.6 1.9 fusion.14
  759.6 1.6 fusion.42
  766.6 5.7 fusion.4
  (112 shorter events, 10.8 us)
Async XLA Ops:
  6.5 203.5 %copy-start = (bf16[8,65536]{1,0:T(8,128)(2,1)S(1)}, bf16[8,65536]{1,0:T(8,128)(2,1)}, u32[]{:S(2)}) copy-start(bf16[8,65536]{1,0:T(8,128)(2,1)} %param.10) | copy-start | bytes 3145732
  6.5 12.5 %copy-start.5 = (s32[24,1]{0,1:T(1,128)S(1)}, s32[24,1]{0,1:T(1,128)}, u32[]{:S(2)}) copy-start(s32[24,1]{0,1:T(1,128)} %param.7) | copy-start | bytes 292
  6.5 12.8 %copy-start.6 = (bf16[24]{0:T(256)(128)(2,1)S(1)}, bf16[24]{0:T(256)(128)(2,1)}, u32[]{:S(2)}) copy-start(bf16[24]{0:T(256)(128)(2,1)} %param.9) | copy-start | bytes 148
  6.5 12.9 %copy-start.7 = (s32[24]{0:T(128)S(1)}, s32[24]{0:T(128)}, u32[]{:S(2)}) copy-start(s32[24]{0:T(128)} %param.8) | copy-start | bytes 292
  10.6 105.2 %all-to-all-start = ((bf16[24,16,4096]{2,0,1:T(8,128)(2,1)}), bf16[24,16,4096]{2,0,1:T(8,128)(2,1)}, u32[]{:S(2)}, u32[]{:S(2)}) async-start(bf16[24,16,4096]{2,0,1:T(8,128)(2,1)} %bitcast.251), calls=%async_computation | async-start | bytes 6291456 | tf_op jit(solution)/shard_map/all_to_all | solution.py:79
  132.8 77.2 %all-to-all-start.1 = ((bf16[8,96,4096]{2,1,0:T(8,128)(2,1)}), bf16[8,96,4096]{2,1,0:T(8,128)(2,1)}, u32[]{:S(2)}, u32[]{:S(2)}) async-start(bf16[8,96,4096]{2,1,0:T(8,128)(2,1)} %copy.175), calls=%async_computation.1 | async-start | bytes 12582912 | tf_op jit(solution)/shard_map/all_to_all | solution.py:91
  138.6 522.4 %all-gather.5.cloned.1.call-start = ((), (), s32[]{:S(2)}) async-start(), calls=%async_computation.2 | async-start | bytes 71303168 | tf_op jit(solution)/shard_map/all_gather | solution.py:115
  267.6 7.0 copy-start.4
  280.3 3.2 copy-start.3
  691.1 5.5 copy-start.2
  763.8 8.6 %copy-start.1 = (bf16[8,65536]{1,0:T(8,128)(2,1)S(1)}, bf16[8,65536]{1,0:T(8,128)(2,1)}, u32[]{:S(2)}) copy-start(bf16[8,65536]{1,0:T(8,128)(2,1)} %param.10) | copy-start | bytes 3145732
Sparse Core Ops, SparseCore 0:
  294.4 366.5 all-gather.4
